TPU v7x, 32 devices: a whole 2x2x4 slice. The times are simulated.
32 devices in a mesh: rows: 4 (over y, core), cols: 8 (over z, x).
Axes of the slice: x: 2, y: 2, z: 4, core: 2. Of those that a mesh axis runs over, the one named last changes fastest.
Arguments:
- prior: float32 [64, 512, 512], P('rows', 'cols'), may hold values from -6 to 6
- obs_cell: int32 [8, 128], replicated, may hold values from 0 to 32767, as said below
- obs_weight: float32 [8, 128, 8], replicated, may hold values from 0.1 to 1
- obs_value: float32 [8, 128], replicated, may hold values from -8 to 8
- obs_var: float32 [8, 128], replicated, may hold values from 0.25 to 4
- loc_mask: int32 [8, 32], replicated, may hold values from 0 to 1, as said below
- batch_order: int32 [8], replicated, may hold values from 0 to 7, each once
- kernel: float32 [8, 7, 7], replicated, may hold values from 0.005 to 0.04
- mixing: float32 [8, 8], replicated, may hold values from -2 to 2
Outputs:
- forecast: float32 [64, 512, 512], P('rows', 'cols')
Inputs may be any that keep to these rules, and one draw needn't show every extreme that they name: `obs_cell`: all 128 cells of one batch lie in one tile, rows r * 16 to (r + 1) * 16 - 1 and columns c * 64 to (c + 1) * 64 - 1, whose index is r * 8 + c. `loc_mask`: for each batch the tiles marked 1 form a rectangle of tiles that contains the tile of that batch's cells. `batch_order`: each batch appears once.
All inputs are finite; a program needn't handle non-finite values.
Results may differ from a plain program's by a relative error of at most 0.0003.
Values sent between devices are 32-bit elements; how exact they have to be, the bound alone decides.
No kernel may reach another device: no remote copies, remote signals or barrier semaphores. Data moves between devices by JAX's collectives and lax.ppermute only.
A program may use at most 128 MiB of HBM per device.

v0:
```python
import jax
import jax.numpy as jnp
from jax import lax
from jax.sharding import PartitionSpec as P

BATCHES = 8
KW = 7
HALFW = 48


def with_halo(shard, sides, width):
    for axis, dim in sides:
        size, length = (lax.axis_size(axis), shard.shape[dim])
        up = [(i, (i + 1) % size) for i in range(size - 1)]
        down = [(j, i) for i, j in up]
        last = lax.slice_in_dim(shard, length - width, length, axis=dim)
        initial = lax.slice_in_dim(shard, 0, width, axis=dim)
        before = lax.ppermute(last, axis, up)
        after = lax.ppermute(initial, axis, down)
        shard = jnp.concatenate([before, shard, after], axis=dim)
    return shard


def taper_weights(ratio):
    clamped = jnp.maximum(ratio, 1.0)
    inner_part = (((-0.25 * ratio + 0.5) * ratio + 0.625) * ratio - 5.0 / 3.0) * ratio * ratio + 1.0
    outer_part = (
        ((((ratio / 12.0 - 0.5) * ratio + 0.625) * ratio + 5.0 / 3.0) * ratio - 5.0) * ratio
        + 4.0
        - 2.0 / (3.0 * clamped)
    )
    return jnp.where(ratio <= 1.0, inner_part, jnp.where(ratio < 2.0, outer_part, 0.0))


def batch_gain(predicted, value_row, var_row):
    mean_pred = jnp.mean(predicted, axis=1)
    spread = predicted - mean_pred[:, None]
    variance = jnp.sum(spread * spread, axis=1) / (predicted.shape[1] - 1)
    denominator = variance + var_row
    shrink = 1.0 / (1.0 + jnp.sqrt(var_row / denominator))
    kalman_gain = ((value_row - mean_pred)[:, None] - shrink[:, None] * spread) / denominator[
        :, None
    ]
    return (spread, kalman_gain)


def refresh_block(block, first_row, first_col, cell_row, cell_col, spread, kalman_gain, active):
    rows_count, cols_count, channels = block.shape
    members = spread.shape[1]
    species = channels // members
    row_pos = (first_row + jnp.arange(rows_count, dtype=jnp.int32)).astype(jnp.float32)
    col_pos = (first_col + jnp.arange(cols_count, dtype=jnp.int32)).astype(jnp.float32)
    row_gap = row_pos[:, None, None] - cell_row.astype(jnp.float32)[None, None, :]
    col_gap = col_pos[None, :, None] - cell_col.astype(jnp.float32)[None, None, :]
    squared = row_gap * row_gap + col_gap * col_gap
    taper = taper_weights(jnp.sqrt(squared) / HALFW) * active
    taper = taper.reshape(rows_count * cols_count, cell_row.shape[0])
    members_view = block.reshape(rows_count * cols_count, species, members)
    covariance = jnp.einsum(
        "psm,im->psi", members_view, spread, precision=lax.Precision.HIGHEST
    ) / (members - 1)
    increment = jnp.einsum(
        "psi,im->psm", covariance * taper[:, None, :], kalman_gain, precision=lax.Precision.HIGHEST
    )
    return (members_view + increment).reshape(rows_count, cols_count, channels)


def refresh_tile(ensemble, row_start, col_start, cell_row, cell_col, spread, kalman_gain, active):
    pieces = refresh_block(
        ensemble, row_start + 0, col_start, cell_row, cell_col, spread, kalman_gain, active
    )
    return pieces


def local_prediction(ensemble, cell_row, cell_col, weights_rows, row_start, col_start):
    tile_height, tile_width, channels = ensemble.shape
    species = weights_rows.shape[1]
    members = channels // species
    local_row = cell_row - row_start
    local_col = cell_col - col_start
    inside = (
        (local_row >= 0) & (local_row < tile_height) & (local_col >= 0) & (local_col < tile_width)
    )
    flat_index = jnp.clip(local_row, 0, tile_height - 1) * tile_width + jnp.clip(
        local_col, 0, tile_width - 1
    )
    picked = ensemble.reshape(tile_height * tile_width, species, members)[flat_index]
    predicted = jnp.einsum("is,ism->im", weights_rows, picked, precision=lax.Precision.HIGHEST)
    return jnp.where(inside[:, None], predicted, 0.0)


def shards(prior, obs_cell, obs_weight, obs_value, obs_var, loc_mask, batch_order, kernel, mixing):
    tile_height, tile_width, channels = prior.shape
    species = kernel.shape[0]
    members = channels // species
    cols_count = lax.axis_size("cols")
    grid_width = tile_width * cols_count
    row_start = lax.axis_index("rows") * tile_height
    col_start = lax.axis_index("cols") * tile_width
    my_tile = lax.axis_index("rows") * cols_count + lax.axis_index("cols")
    ensemble = prior
    for position in range(BATCHES):
        current = batch_order[position]
        obs_cells = obs_cell[current]
        cell_row = obs_cells // grid_width
        cell_col = obs_cells % grid_width
        partial_value = local_prediction(
            ensemble, cell_row, cell_col, obs_weight[current], row_start, col_start
        )
        predicted = lax.psum(partial_value, ("rows", "cols"))
        spread, kalman_gain = batch_gain(predicted, obs_value[current], obs_var[current])
        active = loc_mask[current, my_tile].astype(jnp.float32)
        ensemble = refresh_tile(
            ensemble, row_start, col_start, cell_row, cell_col, spread, kalman_gain, active
        )
    halo_width = KW // 2
    padded = with_halo(ensemble, (("rows", 0), ("cols", 1)), 3)
    padded_width = tile_width + 2 * halo_width
    offsets = (
        jnp.arange(padded_width, dtype=jnp.int32)[None, :]
        - jnp.arange(tile_width, dtype=jnp.int32)[:, None]
    )
    onehot = (offsets[:, :, None] == jnp.arange(KW, dtype=jnp.int32)[None, None, :]).astype(
        jnp.float32
    )
    band_matrix = jnp.einsum("tak,xik->taxi", kernel, onehot, precision=lax.Precision.HIGHEST)
    padded_grid = padded.reshape(tile_height + 2 * halo_width, padded_width, species, members)
    smoothed = jnp.zeros((tile_height, tile_width, species, members), jnp.float32)
    for vertical in range(KW):
        smoothed = smoothed + jnp.einsum(
            "txi,yitm->yxtm",
            band_matrix[:, vertical],
            padded_grid[vertical : vertical + tile_height],
            precision=lax.Precision.HIGHEST,
        )
    mixed_field = jnp.einsum("st,yxtm->yxsm", mixing, smoothed, precision=lax.Precision.HIGHEST)
    return mixed_field.reshape(tile_height, tile_width, channels)


def solution(mesh):
    return jax.shard_map(
        shards,
        mesh=mesh,
        in_specs=(P("rows", "cols", None), P(), P(), P(), P(), P(), P(), P(), P()),
        out_specs=P("rows", "cols", None),
        check_vma=False,
    )
```

profile of v0, /device:TPU:1, one launch (start us, length us, event | category | flops | bytes accessed | tf_op | source)
XLA Modules:
  0.0 676.1 jit_solution(12245388337613379013)
XLA Ops:
  34.7 40.8 %psum.56 = f32[128,64]{0,1:T(8,128)S(1)} all-reduce(f32[128,64]{0,1:T(8,128)S(1)} %broadcast_select_fusion.7), channel_id=1, replica_groups=mesh['rows'=4,'cols'=8] {'rows','cols'}, use_global_device_ids=true, to_apply=%region_0.1 | all-reduce | flops 8192 | bytes 65536 | tf_op jit(solution)/shard_map/psum | solution.py:110
  91.1 40.8 %psum.57 = f32[128,64]{0,1:T(8,128)S(1)} all-reduce(f32[128,64]{0,1:T(8,128)S(1)} %broadcast_select_fusion.6), channel_id=1, replica_groups=mesh['rows'=4,'cols'=8] {'rows','cols'}, use_global_device_ids=true, to_apply=%region_3.4 | all-reduce | flops 8192 | bytes 65536 | tf_op jit(solution)/shard_map/psum | solution.py:110
  131.9 6.8 %fusion.242 = f32[1024,8,128]{2,0,1:T(8,128)S(1)} fusion(f32[1024,8,64]{0,2,1:T(8,128)S(1)} %fusion.60, f32[128,64]{0,1:T(8,128)S(1)} %psum.57, f32[128]{0:T(128)S(1)} %get-tuple-element.169), kind=kOutput, calls=%fused_computation.329 | convolution fusion | flops 805314560 | bytes 6324736 | tf_op jit(solution)/shard_map/psm,im->psi/dot_general | solution.py:59
  153.8 40.1 %psum.58 = f32[128,64]{0,1:T(8,128)S(1)} all-reduce(f32[128,64]{0,1:T(8,128)S(1)} %broadcast_select_fusion.5), channel_id=1, replica_groups=mesh['rows'=4,'cols'=8] {'rows','cols'}, use_global_device_ids=true, to_apply=%region_6.7 | all-reduce | flops 8192 | bytes 65536 | tf_op jit(solution)/shard_map/psum | solution.py:110
  194.1 6.8 %fusion.239 = f32[1024,8,128]{2,0,1:T(8,128)S(1)} fusion(f32[1024,8,64]{0,2,1:T(8,128)S(1)} %copy-done.2, f32[128,64]{0,1:T(8,128)S(1)} %psum.58, f32[128]{0:T(128)S(1)} %get-tuple-element.167), kind=kOutput, calls=%fused_computation.326 | convolution fusion | flops 805314560 | bytes 6324736 | tf_op jit(solution)/shard_map/psm,im->psi/dot_general | solution.py:59
  216.3 40.2 %psum.59 = f32[128,64]{0,1:T(8,128)S(1)} all-reduce(f32[128,64]{0,1:T(8,128)S(1)} %broadcast_select_fusion.4), channel_id=1, replica_groups=mesh['rows'=4,'cols'=8] {'rows','cols'}, use_global_device_ids=true, to_apply=%region_9.10 | all-reduce | flops 8192 | bytes 65536 | tf_op jit(solution)/shard_map/psum | solution.py:110
  256.6 6.8 %fusion.236 = f32[1024,8,128]{2,0,1:T(8,128)S(1)} fusion(f32[1024,8,64]{0,2,1:T(8,128)S(1)} %copy-done.3, f32[128,64]{0,1:T(8,128)S(1)} %psum.59, f32[128]{0:T(128)S(1)} %get-tuple-element.165), kind=kOutput, calls=%fused_computation.323 | convolution fusion | flops 805314560 | bytes 6324736 | tf_op jit(solution)/shard_map/psm,im->psi/dot_general | solution.py:59
  278.6 40.1 %psum.60 = f32[128,64]{0,1:T(8,128)S(1)} all-reduce(f32[128,64]{0,1:T(8,128)S(1)} %broadcast_select_fusion.3), channel_id=1, replica_groups=mesh['rows'=4,'cols'=8] {'rows','cols'}, use_global_device_ids=true, to_apply=%region_12.13 | all-reduce | flops 8192 | bytes 65536 | tf_op jit(solution)/shard_map/psum | solution.py:110
  318.8 6.8 %fusion.233 = f32[1024,8,128]{2,0,1:T(8,128)S(1)} fusion(f32[1024,8,64]{0,2,1:T(8,128)S(1)} %copy-done.4, f32[128,64]{0,1:T(8,128)S(1)} %psum.60, f32[128]{0:T(128)S(1)} %get-tuple-element.163), kind=kOutput, calls=%fused_computation.320 | convolution fusion | flops 805314560 | bytes 6324736 | tf_op jit(solution)/shard_map/psm,im->psi/dot_general | solution.py:59
  327.0 6.3 fusion.48
  341.0 40.2 %psum.61 = f32[128,64]{0,1:T(8,128)S(1)} all-reduce(f32[128,64]{0,1:T(8,128)S(1)} %broadcast_select_fusion.2), channel_id=1, replica_groups=mesh['rows'=4,'cols'=8] {'rows','cols'}, use_global_device_ids=true, to_apply=%region_15.16 | all-reduce | flops 8192 | bytes 65536 | tf_op jit(solution)/shard_map/psum | solution.py:110
  381.4 6.8 %fusion.230 = f32[1024,8,128]{2,0,1:T(8,128)S(1)} fusion(f32[1024,8,64]{0,2,1:T(8,128)S(1)} %copy-done.5, f32[128,64]{0,1:T(8,128)S(1)} %psum.61, f32[128]{0:T(128)S(1)} %get-tuple-element.161), kind=kOutput, calls=%fused_computation.317 | convolution fusion | flops 805314560 | bytes 6324736 | tf_op jit(solution)/shard_map/psm,im->psi/dot_general | solution.py:59
  403.2 40.3 %psum.62 = f32[128,64]{0,1:T(8,128)S(1)} all-reduce(f32[128,64]{0,1:T(8,128)S(1)} %broadcast_select_fusion.1), channel_id=1, replica_groups=mesh['rows'=4,'cols'=8] {'rows','cols'}, use_global_device_ids=true, to_apply=%region_18.19 | all-reduce | flops 8192 | bytes 65536 | tf_op jit(solution)/shard_map/psum | solution.py:110
  443.5 6.8 %fusion.227 = f32[1024,8,128]{2,0,1:T(8,128)S(1)} fusion(f32[1024,8,64]{0,2,1:T(8,128)S(1)} %copy-done.6, f32[128,64]{0,1:T(8,128)S(1)} %psum.62, f32[128]{0:T(128)S(1)} %get-tuple-element.159), kind=kOutput, calls=%fused_computation.314 | convolution fusion | flops 805314560 | bytes 6324736 | tf_op jit(solution)/shard_map/psm,im->psi/dot_general | solution.py:59
  462.7 40.7 %psum.63 = f32[128,64]{0,1:T(8,128)S(1)} all-reduce(f32[128,64]{0,1:T(8,128)S(1)} %broadcast_select_fusion), channel_id=1, replica_groups=mesh['rows'=4,'cols'=8] {'rows','cols'}, use_global_device_ids=true, to_apply=%region_21.22 | all-reduce | flops 8192 | bytes 65536 | tf_op jit(solution)/shard_map/psum | solution.py:110
  503.5 6.8 %fusion.224 = f32[1024,8,128]{2,0,1:T(8,128)S(1)} fusion(f32[1024,8,64]{0,2,1:T(8,128)S(1)} %fusion.54, f32[128,64]{0,1:T(8,128)S(1)} %psum.63, f32[128]{0:T(128)S(1)} %get-tuple-element.133), kind=kOutput, calls=%fused_computation.311 | convolution fusion | flops 805314560 | bytes 6324736 | tf_op jit(solution)/shard_map/psm,im->psi/dot_general | solution.py:59
  583.9 10.3 %fusion.10 = f32[8,16,64,64]{3,2,1,0:T(8,128)S(1)} fusion(f32[16,70,8,64]{3,2,1,0:T(8,128)} %reshape.2901, f32[8,64,70,1]{2,0,1,3:T(8,128)} %get-tuple-element.61), kind=kOutput, calls=%fused_computation.18 | convolution fusion | flops 440401920 | bytes 4534272 | tf_op jit(solution)/shard_map/txi,yitm->yxtm/dot_general | solution.py:130
  594.2 11.8 %fusion.12 = f32[8,16,64,64]{3,2,1,0:T(8,128)} fusion(f32[16,70,8,64]{3,2,1,0:T(8,128)} %reshape.2900, f32[8,64,70,1]{2,0,1,3:T(8,128)S(1)} %copy-done.17), kind=kOutput, calls=%fused_computation.20 | convolution fusion | flops 440401920 | bytes 4534272 | tf_op jit(solution)/shard_map/txi,yitm->yxtm/dot_general | solution.py:130
  606.1 9.4 %fusion.2 = f32[8,16,64,64]{3,2,1,0:T(8,128)} fusion(f32[16,70,8,64]{3,2,1,0:T(8,128)S(1)} %bitcast.856, f32[8,64,70,1]{2,0,1,3:T(8,128)S(1)} %copy-done.16), kind=kOutput, calls=%fused_computation.10 | convolution fusion | flops 440401920 | bytes 4534272 | tf_op jit(solution)/shard_map/txi,yitm->yxtm/dot_general | solution.py:130
  615.5 9.9 %fusion.4 = f32[8,16,64,64]{3,2,1,0:T(8,128)} fusion(f32[16,70,8,64]{3,2,1,0:T(8,128)S(1)} %bitcast.854, f32[8,64,70,1]{2,0,1,3:T(8,128)S(1)} %copy-done.15), kind=kOutput, calls=%fused_computation.12 | convolution fusion | flops 440401920 | bytes 4534272 | tf_op jit(solution)/shard_map/txi,yitm->yxtm/dot_general | solution.py:130
  625.4 9.5 %fusion.6 = f32[8,16,64,64]{3,2,1,0:T(8,128)} fusion(f32[16,70,8,64]{3,2,1,0:T(8,128)S(1)} %bitcast.852, f32[8,64,70,1]{2,0,1,3:T(8,128)S(1)} %copy-done.14), kind=kOutput, calls=%fused_computation.14 | convolution fusion | flops 440401920 | bytes 4534272 | tf_op jit(solution)/shard_map/txi,yitm->yxtm/dot_general | solution.py:130
  635.0 9.4 %fusion.8 = f32[8,16,64,64]{3,2,1,0:T(8,128)} fusion(f32[16,70,8,64]{3,2,1,0:T(8,128)S(1)} %bitcast.850, f32[8,64,70,1]{2,0,1,3:T(8,128)S(1)} %get-tuple-element.60), kind=kOutput, calls=%fused_computation.16 | convolution fusion | flops 440401920 | bytes 4534272 | tf_op jit(solution)/shard_map/txi,yitm->yxtm/dot_general | solution.py:130
  644.4 13.5 %add_bitcast_fusion = f32[16,64,8,64]{1,3,0,2:T(8,128)} fusion(f32[8,16,64,64]{3,2,1,0:T(8,128)S(1)} %copy-done.10, f32[8,16,64,64]{3,2,1,0:T(8,128)} %fusion.4, f32[8,16,64,64]{3,2,1,0:T(8,128)} %fusion.6, f32[8,16,64,64]{3,2,1,0:T(8,128)} %fusion.8, f32[8,16,64,64]{3,2,1,0:T(8,128)S(1)} %copy-done.9, f32[8,16,64,64]{3,2,1,0:T(8,128)S(1)} %fusion.10, ...), kind=kOutput, calls=%fused_computation.24 | convolution fusion | flops 443547648 | bytes 17117184 | tf_op jit(solution)/shard_map/txi,yitm->yxtm/dot_general | solution.py:130
  663.3 7.8 %convolution_bitcast_fusion = f32[16,64,8,64]{3,2,1,0:T(8,128)} fusion(f32[16,64,8,64]{3,2,1,0:T(8,128)} %copy.99, f32[8,8]{1,0:T(8,128)S(1)} %copy-done.45), kind=kOutput, calls=%fused_computation.40 | convolution fusion | flops 50331648 | bytes 4194560 | tf_op jit(solution)/shard_map/st,yxtm->yxsm/dot_general | solution.py:136
  (314 shorter events, 195.7 us)
Async XLA Ops:
  0.0 534.7 %copy-start = (f32[8,7,7]{2,0,1:T(8,128)S(1)}, f32[8,7,7]{2,0,1:T(8,128)}, u32[]{:S(2)}) copy-start(f32[8,7,7]{2,0,1:T(8,128)} %param.16) | copy-start | bytes 4708
  0.0 24.1 %copy-start.13 = (f32[16,64,512]{2,1,0:T(8,128)S(1)}, f32[16,64,512]{2,1,0:T(8,128)}, u32[]{:S(2)}) copy-start(f32[16,64,512]{2,1,0:T(8,128)} %param.9) | copy-start | bytes 6291460
  29.4 50.4 %copy-start.8 = (f32[1024,8,64]{0,2,1:T(8,128)}, f32[1024,8,64]{0,2,1:T(8,128)S(1)}, u32[]{:S(2)}) copy-start(f32[1024,8,64]{0,2,1:T(8,128)S(1)} %copy.67) | copy-start | bytes 6291460
  85.0 46.9 %copy-start.46 = (f32[8,128]{1,0:T(8,128)S(1)}, f32[8,128]{1,0:T(8,128)}, u32[]{:S(2)}) copy-start(f32[8,128]{1,0:T(8,128)} %param.12) | copy-start | bytes 12292
  87.7 51.0 %copy-start.47 = (f32[8,128]{1,0:T(8,128)S(1)}, f32[8,128]{1,0:T(8,128)}, u32[]{:S(2)}) copy-start(f32[8,128]{1,0:T(8,128)} %param.13) | copy-start | bytes 12292
  87.8 51.6 %copy-start.22 = (f32[16,128]{1,0:T(8,128)S(1)}, f32[16,128]{1,0:T(8,128)}, u32[]{:S(2)}) copy-start(f32[16,128]{1,0:T(8,128)} %get-tuple-element.135) | copy-start | bytes 24580
  146.4 47.7 %copy-start.2 = (f32[1024,8,64]{0,2,1:T(8,128)S(1)}, f32[1024,8,64]{0,2,1:T(8,128)}, u32[]{:S(2)}) copy-start(f32[1024,8,64]{0,2,1:T(8,128)} %fusion.39) | copy-start | bytes 6291460
  150.5 51.0 %copy-start.21 = (f32[16,128]{1,0:T(8,128)S(1)}, f32[16,128]{1,0:T(8,128)}, u32[]{:S(2)}) copy-start(f32[16,128]{1,0:T(8,128)} %get-tuple-element.136) | copy-start | bytes 24580
  208.6 48.0 %copy-start.3 = (f32[1024,8,64]{0,2,1:T(8,128)S(1)}, f32[1024,8,64]{0,2,1:T(8,128)}, u32[]{:S(2)}) copy-start(f32[1024,8,64]{0,2,1:T(8,128)} %fusion.42) | copy-start | bytes 6291460
  213.0 51.1 %copy-start.20 = (f32[16,128]{1,0:T(8,128)S(1)}, f32[16,128]{1,0:T(8,128)}, u32[]{:S(2)}) copy-start(f32[16,128]{1,0:T(8,128)} %get-tuple-element.137) | copy-start | bytes 24580
  271.1 47.7 %copy-start.4 = (f32[1024,8,64]{0,2,1:T(8,128)S(1)}, f32[1024,8,64]{0,2,1:T(8,128)}, u32[]{:S(2)}) copy-start(f32[1024,8,64]{0,2,1:T(8,128)} %fusion.45) | copy-start | bytes 6291460
  275.3 51.0 %copy-start.19 = (f32[16,128]{1,0:T(8,128)S(1)}, f32[16,128]{1,0:T(8,128)}, u32[]{:S(2)}) copy-start(f32[16,128]{1,0:T(8,128)} %get-tuple-element.138) | copy-start | bytes 24580
  333.3 48.0 %copy-start.5 = (f32[1024,8,64]{0,2,1:T(8,128)S(1)}, f32[1024,8,64]{0,2,1:T(8,128)}, u32[]{:S(2)}) copy-start(f32[1024,8,64]{0,2,1:T(8,128)} %fusion.48) | copy-start | bytes 6291460
  337.7 51.1 %copy-start.18 = (f32[16,128]{1,0:T(8,128)S(1)}, f32[16,128]{1,0:T(8,128)}, u32[]{:S(2)}) copy-start(f32[16,128]{1,0:T(8,128)} %get-tuple-element.139) | copy-start | bytes 24580
  395.8 47.6 %copy-start.6 = (f32[1024,8,64]{0,2,1:T(8,128)S(1)}, f32[1024,8,64]{0,2,1:T(8,128)}, u32[]{:S(2)}) copy-start(f32[1024,8,64]{0,2,1:T(8,128)} %fusion.51) | copy-start | bytes 6291460
  521.4 14.1 %collective-permute-start = (f32[3,64,512]{2,1,0:T(8,128)}, f32[3,64,512]{2,1,0:T(8,128)}, u32[]{:S(2)}, u32[]{:S(2)}) collective-permute-start(f32[3,64,512]{2,1,0:T(8,128)} %slice.114), channel_id=1, source_target_pairs={{0,8},{8,16},{16,24},{1,9},{9,17},{17,25},{2,10},{10,18},{18,26},{... | collective-permute-start | bytes 1179656 | tf_op jit(solution)/shard_map/ppermute | solution.py:18
  527.4 9.1 %collective-permute-start.1 = (f32[3,64,512]{2,1,0:T(8,128)S(1)}, f32[3,64,512]{2,1,0:T(8,128)S(1)}, u32[]{:S(2)}, u32[]{:S(2)}) collective-permute-start(f32[3,64,512]{2,1,0:T(8,128)S(1)} %slice.116), channel_id=1, source_target_pairs={{8,0},{16,8},{24,16},{9,1},{17,9},{25,17},{10,2},{18,10},{26,18},{... | collective-permute-start | bytes 1179656 | tf_op jit(solution)/shard_map/ppermute | solution.py:19
  537.4 9.4 %collective-permute-start.2 = (f32[22,3,512]{2,1,0:T(4,128)S(1)}, f32[22,3,512]{2,1,0:T(4,128)S(1)}, u32[]{:S(2)}, u32[]{:S(2)}) collective-permute-start(f32[22,3,512]{2,1,0:T(4,128)S(1)} %get-tuple-element.52), channel_id=1, source_target_pairs={{0,1},{1,2},{2,3},{3,4},{4,5},{5,6},{6,7},{8,9},{9,10},{10,11},{11... | collective-permute-start | bytes 405512 | tf_op jit(solution)/shard_map/ppermute | solution.py:18
  540.5 6.4 collective-permute-start.3
  581.3 24.8 %slice-start.6 = ((s8[4587520]{0:T(1024)(128)(4,1)}), s8[393216]{0:T(1024)(128)(4,1)S(1)}, s32[]{:S(2)}) async-start(s8[4587520]{0:T(1024)(128)(4,1)} %bitcast.855), calls=%async_computation.6 | async-start | bytes 786432
  583.9 22.2 %slice-start.7 = ((s8[4587520]{0:T(1024)(128)(4,1)}), s8[4194304]{0:T(1024)(128)(4,1)S(1)}, s32[]{:S(2)}) async-start(s8[4587520]{0:T(1024)(128)(4,1)} %bitcast.855), calls=%async_computation.7 | async-start | bytes 8388608
  594.2 21.3 %slice-start.4 = ((s8[4587520]{0:T(1024)(128)(4,1)}), s8[4194304]{0:T(1024)(128)(4,1)S(1)}, s32[]{:S(2)}) async-start(s8[4587520]{0:T(1024)(128)(4,1)} %bitcast.853), calls=%async_computation.4 | async-start | bytes 8388608
  594.2 31.2 %slice-start.2 = ((s8[4587520]{0:T(1024)(128)(4,1)}), s8[4194304]{0:T(1024)(128)(4,1)S(1)}, s32[]{:S(2)}) async-start(s8[4587520]{0:T(1024)(128)(4,1)} %bitcast.851), calls=%async_computation.2 | async-start | bytes 8388608
  615.5 19.4 %slice-start = ((s8[4587520]{0:T(1024)(128)(4,1)}), s8[4194304]{0:T(1024)(128)(4,1)S(1)}, s32[]{:S(2)}) async-start(s8[4587520]{0:T(1024)(128)(4,1)} %bitcast.849), calls=%async_computation | async-start | bytes 8388608
  (52 other events, 353.9 us)
where the time goes:
time: 687 us; the launch traced here: 676 us
  blocking collectives  323 us (47%)
  matrix products  179 us (26%)
  local copies, waits for them, and re-layouts  118 us (17%)
  between operations  21.8 us (3%)
  other arithmetic  17 us (2%)
  starting transfers between devices  11.7 us (2%)
    psum x8, blocking collectives, shards(): predicted = lax.psum(partial_value, ('rows', 'cols'))  323 us
    dot_general x7, matrix products, shards(): jnp.einsum('txi,yitm->yxtm', band_matrix[:, vertical], padded_grid[vertic...  73.8 us
    dot_general x8, matrix products, refresh_block(): jnp.einsum('psm,im->psi', members_view, spread, precision=lax.Precision.H...  50.9 us
    dot_general x8, matrix products, refresh_block(): jnp.einsum('psi,im->psm', covariance * taper[:, None, :], kalman_gain, pr...  45.7 us
    slice x8, local copies, waits for them, and re-layouts, shards(): padded_grid[vertical:vertical + tile_height]  35.5 us
    add x7, local copies, waits for them, and re-layouts, refresh_block(): return (members_view + increment).reshape(rows_count, cols_count, channels)  26.4 us
    gather x8, local copies, waits for them, and re-layouts, local_prediction(): ensemble.reshape(tile_height * tile_width, species, members)[flat_index]  23.4 us
  transfers between devices with their start and end apart: 4, of which 3 were waited for; matrix products, arithmetic and copies ran while one was open for 1% of the time, Pallas kernels for 0%

commit v1 on v0

--- a/solution.py
+++ b/solution.py
@@ -107,7 +107,7 @@
         partial_value = local_prediction(
             ensemble, cell_row, cell_col, obs_weight[current], row_start, col_start
         )
-        predicted = lax.psum(partial_value, ("rows", "cols"))
+        predicted = jnp.sum(lax.all_gather(partial_value, ("rows", "cols")), axis=0)
         spread, kalman_gain = batch_gain(predicted, obs_value[current], obs_var[current])
         active = loc_mask[current, my_tile].astype(jnp.float32)
         ensemble = refresh_tile(

time: 687 us -> 802 us (1.17)
  waiting for transfers between devices: 4.9 us -> 411 us
  blocking collectives: 323 us -> 0 us
  between operations: 21.8 us -> 34.8 us
  other arithmetic: 17 us -> 28 us
    all_gather x0 -> x8, waiting for transfers between devices: none -> 405 us  [shards(): predicted = jnp.sum(lax.all_gather(partial_value, ('rows', 'cols')), axis=0)]
    psum x8 -> x0, blocking collectives: 323 us -> none  [shards(): predicted = lax.psum(partial_value, ('rows', 'cols'))]
    unnamed x152 -> x96, local copies, waits for them, and re-layouts: 2.52 us -> 13.6 us
    reduce_sum x8 -> x16, other arithmetic: 0.2 us -> 10.5 us  [batch_gain(): mean_pred = jnp.mean(predicted, axis=1)]
  transfers between devices with their start and end apart: 4 -> 12, of which waited for: 3 -> 10; matrix products, arithmetic and copies ran while one was open for 1% -> 2% of each run, Pallas kernels for 0% -> 0%
where the time goes in v1:
time: 802 us; the launch traced here: 792 us
  waiting for transfers between devices  411 us (51%)
  matrix products  179 us (22%)
  local copies, waits for them, and re-layouts  126 us (16%)
  between operations  34.8 us (4%)
  other arithmetic  28 us (3%)
  starting transfers between devices  11.6 us (1%)
    all_gather x8, waiting for transfers between devices, shards(): predicted = jnp.sum(lax.all_gather(partial_value, ('rows', 'cols')), axis=0)  405 us
    dot_general x7, matrix products, shards(): jnp.einsum('txi,yitm->yxtm', band_matrix[:, vertical], padded_grid[vertic...  73.7 us
    dot_general x8, matrix products, refresh_block(): jnp.einsum('psm,im->psi', members_view, spread, precision=lax.Precision.H...  50.9 us
    dot_general x8, matrix products, refresh_block(): jnp.einsum('psi,im->psm', covariance * taper[:, None, :], kalman_gain, pr...  45 us
    slice x8, local copies, waits for them, and re-layouts, shards(): padded_grid[vertical:vertical + tile_height]  35.4 us
    add x7, local copies, waits for them, and re-layouts, refresh_block(): return (members_view + increment).reshape(rows_count, cols_count, channels)  23.8 us
    gather x8, local copies, waits for them, and re-layouts, local_prediction(): ensemble.reshape(tile_height * tile_width, species, members)[flat_index]  22.6 us
  transfers between devices with their start and end apart: 12, of which 10 were waited for; matrix products, arithmetic and copies ran while one was open for 2% of the time, Pallas kernels for 0%

profile of v1, /device:TPU:1, one launch (start us, length us, event | category | flops | bytes accessed | tf_op | source)
XLA Modules:
  0.0 791.5 jit_solution(15654982182627190231)
XLA Ops:
  37.9 49.4 %all-gather.17.cloned.1.call-done = f32[4096,64]{0,1:T(8,128)} async-done(((f32[128,64]{0,1:T(8,128)}), f32[4096,64]{0,1:T(8,128)}) %all-gather.17.cloned.1.call-update) | async-done | bytes 1048592 | tf_op jit(solution)/shard_map/all_gather | solution.py:110
  106.7 50.6 %all-gather.19.cloned.1.call-done = f32[4096,64]{0,1:T(8,128)} async-done(((f32[128,64]{0,1:T(8,128)}), f32[4096,64]{0,1:T(8,128)}) %all-gather.19.cloned.1.call-update) | async-done | bytes 1048592 | tf_op jit(solution)/shard_map/all_gather | solution.py:110
  160.2 6.8 fusion.242
  167.1 6.3 fusion.39
  182.7 50.8 %all-gather.21.cloned.1.call-done = f32[4096,64]{0,1:T(8,128)} async-done(((f32[128,64]{0,1:T(8,128)}), f32[4096,64]{0,1:T(8,128)}) %all-gather.21.cloned.1.call-update) | async-done | bytes 1048592 | tf_op jit(solution)/shard_map/all_gather | solution.py:110
  236.5 6.8 fusion.239
  256.8 50.6 %all-gather.23.cloned.1.call-done = f32[4096,64]{0,1:T(8,128)} async-done(((f32[128,64]{0,1:T(8,128)}), f32[4096,64]{0,1:T(8,128)}) %all-gather.23.cloned.1.call-update) | async-done | bytes 1048592 | tf_op jit(solution)/shard_map/all_gather | solution.py:110
  310.3 6.8 fusion.236
  332.8 50.8 %all-gather.25.cloned.1.call-done = f32[4096,64]{0,1:T(8,128)} async-done(((f32[128,64]{0,1:T(8,128)}), f32[4096,64]{0,1:T(8,128)}) %all-gather.25.cloned.1.call-update) | async-done | bytes 1048592 | tf_op jit(solution)/shard_map/all_gather | solution.py:110
  386.5 6.8 fusion.233
  406.8 50.6 %all-gather.27.cloned.1.call-done = f32[4096,64]{0,1:T(8,128)} async-done(((f32[128,64]{0,1:T(8,128)}), f32[4096,64]{0,1:T(8,128)}) %all-gather.27.cloned.1.call-update) | async-done | bytes 1048592 | tf_op jit(solution)/shard_map/all_gather | solution.py:110
  460.3 6.8 fusion.230
  482.8 50.8 %all-gather.29.cloned.1.call-done = f32[4096,64]{0,1:T(8,128)} async-done(((f32[128,64]{0,1:T(8,128)}), f32[4096,64]{0,1:T(8,128)}) %all-gather.29.cloned.1.call-update) | async-done | bytes 1048592 | tf_op jit(solution)/shard_map/all_gather | solution.py:110
  536.5 6.8 fusion.227
  559.0 51.2 %all-gather.31.cloned.1.call-done = f32[4096,64]{0,1:T(8,128)} async-done(((f32[128,64]{0,1:T(8,128)}), f32[4096,64]{0,1:T(8,128)}) %all-gather.31.cloned.1.call-update) | async-done | bytes 1048592 | tf_op jit(solution)/shard_map/all_gather | solution.py:110
  613.1 6.8 fusion.224
  692.6 10.3 %fusion.10 = f32[8,16,64,64]{3,2,1,0:T(8,128)S(1)} fusion(f32[16,70,8,64]{3,2,1,0:T(8,128)} %reshape.2917, f32[8,64,70,1]{2,0,1,3:T(8,128)} %get-tuple-element.61), kind=kOutput, calls=%fused_computation.18 | convolution fusion | flops 440401920 | bytes 4534272 | tf_op jit(solution)/shard_map/txi,yitm->yxtm/dot_general | solution.py:130
  702.9 11.8 %fusion.12 = f32[8,16,64,64]{3,2,1,0:T(8,128)} fusion(f32[16,70,8,64]{3,2,1,0:T(8,128)} %reshape.2916, f32[8,64,70,1]{2,0,1,3:T(8,128)S(1)} %copy-done.17), kind=kOutput, calls=%fused_computation.20 | convolution fusion | flops 440401920 | bytes 4534272 | tf_op jit(solution)/shard_map/txi,yitm->yxtm/dot_general | solution.py:130
  714.8 9.4 %fusion.2 = f32[8,16,64,64]{3,2,1,0:T(8,128)} fusion(f32[16,70,8,64]{3,2,1,0:T(8,128)S(1)} %bitcast.912, f32[8,64,70,1]{2,0,1,3:T(8,128)S(1)} %copy-done.16), kind=kOutput, calls=%fused_computation.10 | convolution fusion | flops 440401920 | bytes 4534272 | tf_op jit(solution)/shard_map/txi,yitm->yxtm/dot_general | solution.py:130
  724.2 9.9 %fusion.4 = f32[8,16,64,64]{3,2,1,0:T(8,128)} fusion(f32[16,70,8,64]{3,2,1,0:T(8,128)S(1)} %bitcast.910, f32[8,64,70,1]{2,0,1,3:T(8,128)S(1)} %copy-done.15), kind=kOutput, calls=%fused_computation.12 | convolution fusion | flops 440401920 | bytes 4534272 | tf_op jit(solution)/shard_map/txi,yitm->yxtm/dot_general | solution.py:130
  734.1 9.5 %fusion.6 = f32[8,16,64,64]{3,2,1,0:T(8,128)} fusion(f32[16,70,8,64]{3,2,1,0:T(8,128)S(1)} %bitcast.908, f32[8,64,70,1]{2,0,1,3:T(8,128)S(1)} %copy-done.14), kind=kOutput, calls=%fused_computation.14 | convolution fusion | flops 440401920 | bytes 4534272 | tf_op jit(solution)/shard_map/txi,yitm->yxtm/dot_general | solution.py:130
  743.7 9.4 %fusion.8 = f32[8,16,64,64]{3,2,1,0:T(8,128)} fusion(f32[16,70,8,64]{3,2,1,0:T(8,128)S(1)} %bitcast.906, f32[8,64,70,1]{2,0,1,3:T(8,128)S(1)} %get-tuple-element.60), kind=kOutput, calls=%fused_computation.16 | convolution fusion | flops 440401920 | bytes 4534272 | tf_op jit(solution)/shard_map/txi,yitm->yxtm/dot_general | solution.py:130
  753.1 13.5 %add_bitcast_fusion = f32[16,64,8,64]{1,3,0,2:T(8,128)} fusion(f32[8,16,64,64]{3,2,1,0:T(8,128)S(1)} %copy-done.10, f32[8,16,64,64]{3,2,1,0:T(8,128)} %fusion.4, f32[8,16,64,64]{3,2,1,0:T(8,128)} %fusion.6, f32[8,16,64,64]{3,2,1,0:T(8,128)} %fusion.8, f32[8,16,64,64]{3,2,1,0:T(8,128)S(1)} %copy-done.9, f32[8,16,64,64]{3,2,1,0:T(8,128)S(1)} %fusion.10, ...), kind=kOutput, calls=%fused_computation.24 | convolution fusion | flops 443547648 | bytes 17117184 | tf_op jit(solution)/shard_map/txi,yitm->yxtm/dot_general | solution.py:130
  771.9 7.8 convolution_bitcast_fusion
  (286 shorter events, 216.5 us)
Async XLA Ops:
  6.5 629.0 %copy-start = (f32[8,7,7]{2,0,1:T(8,128)S(1)}, f32[8,7,7]{2,0,1:T(8,128)}, u32[]{:S(2)}) copy-start(f32[8,7,7]{2,0,1:T(8,128)} %param.16) | copy-start | bytes 4708
  6.5 21.0 %copy-start.18 = (f32[8,128,8]{1,2,0:T(8,128)S(1)}, f32[8,128,8]{1,2,0:T(8,128)}, u32[]{:S(2)}) copy-start(f32[8,128,8]{1,2,0:T(8,128)} %param.11) | copy-start | bytes 98308
  6.5 80.8 %all-gather.17.cloned.1.call-start = ((), (), s32[]{:S(2)}) async-start(), calls=%async_computation | async-start | bytes 1081344 | tf_op jit(solution)/shard_map/all_gather | solution.py:110
  32.2 125.2 %all-gather.19.cloned.1.call-start = ((), (), s32[]{:S(2)}) async-start(), calls=%async_computation.1 | async-start | bytes 1081344 | tf_op jit(solution)/shard_map/all_gather | solution.py:110
  35.1 55.1 %copy-start.8 = (f32[1024,8,64]{0,2,1:T(8,128)}, f32[1024,8,64]{0,2,1:T(8,128)S(1)}, u32[]{:S(2)}) copy-start(f32[1024,8,64]{0,2,1:T(8,128)S(1)} %copy.104) | copy-start | bytes 6291460
  36.8 53.3 %copy-start.22 = (f32[8,128]{1,0:T(8,128)S(1)}, f32[8,128]{1,0:T(8,128)}, u32[]{:S(2)}) copy-start(f32[8,128]{1,0:T(8,128)} %param.12) | copy-start | bytes 12292
  104.8 128.8 %all-gather.21.cloned.1.call-start = ((), (), s32[]{:S(2)}) async-start(), calls=%async_computation.2 | async-start | bytes 1081344 | tf_op jit(solution)/shard_map/all_gather | solution.py:110
  180.3 56.2 %copy-start.3 = (f32[1024,8,64]{0,2,1:T(8,128)S(1)}, f32[1024,8,64]{0,2,1:T(8,128)}, u32[]{:S(2)}) copy-start(f32[1024,8,64]{0,2,1:T(8,128)} %fusion.39) | copy-start | bytes 6291460
  181.0 126.4 %all-gather.23.cloned.1.call-start = ((), (), s32[]{:S(2)}) async-start(), calls=%async_computation.3 | async-start | bytes 1081344 | tf_op jit(solution)/shard_map/all_gather | solution.py:110
  254.8 128.8 %all-gather.25.cloned.1.call-start = ((), (), s32[]{:S(2)}) async-start(), calls=%async_computation.4 | async-start | bytes 1081344 | tf_op jit(solution)/shard_map/all_gather | solution.py:110
  330.3 56.2 %copy-start.5 = (f32[1024,8,64]{0,2,1:T(8,128)S(1)}, f32[1024,8,64]{0,2,1:T(8,128)}, u32[]{:S(2)}) copy-start(f32[1024,8,64]{0,2,1:T(8,128)} %fusion.45) | copy-start | bytes 6291460
  331.0 126.4 %all-gather.27.cloned.1.call-start = ((), (), s32[]{:S(2)}) async-start(), calls=%async_computation.5 | async-start | bytes 1081344 | tf_op jit(solution)/shard_map/all_gather | solution.py:110
  404.9 128.8 %all-gather.29.cloned.1.call-start = ((), (), s32[]{:S(2)}) async-start(), calls=%async_computation.6 | async-start | bytes 1081344 | tf_op jit(solution)/shard_map/all_gather | solution.py:110
  480.3 56.2 %copy-start.2 = (f32[1024,8,64]{0,2,1:T(8,128)S(1)}, f32[1024,8,64]{0,2,1:T(8,128)}, u32[]{:S(2)}) copy-start(f32[1024,8,64]{0,2,1:T(8,128)} %fusion.51) | copy-start | bytes 6291460
  481.1 129.2 %all-gather.31.cloned.1.call-start = ((), (), s32[]{:S(2)}) async-start(), calls=%async_computation.7 | async-start | bytes 1081344 | tf_op jit(solution)/shard_map/all_gather | solution.py:110
  557.0 56.2 %copy-start.7 = (f32[1024,8,64]{0,2,1:T(8,128)S(1)}, f32[1024,8,64]{0,2,1:T(8,128)}, u32[]{:S(2)}) copy-start(f32[1024,8,64]{0,2,1:T(8,128)} %fusion.54) | copy-start | bytes 6291460
  629.9 13.1 %collective-permute-start = (f32[3,64,512]{2,1,0:T(8,128)}, f32[3,64,512]{2,1,0:T(8,128)}, u32[]{:S(2)}, u32[]{:S(2)}) collective-permute-start(f32[3,64,512]{2,1,0:T(8,128)} %slice.114), channel_id=1, source_target_pairs={{0,8},{8,16},{16,24},{1,9},{9,17},{17,25},{2,10},{10,18},{18,26},{... | collective-permute-start | bytes 1179656 | tf_op jit(solution)/shard_map/ppermute | solution.py:18
  633.6 9.4 %collective-permute-start.1 = (f32[3,64,512]{2,1,0:T(8,128)S(1)}, f32[3,64,512]{2,1,0:T(8,128)S(1)}, u32[]{:S(2)}, u32[]{:S(2)}) collective-permute-start(f32[3,64,512]{2,1,0:T(8,128)S(1)} %slice.116), channel_id=1, source_target_pairs={{8,0},{16,8},{24,16},{9,1},{17,9},{25,17},{10,2},{18,10},{26,18},{... | collective-permute-start | bytes 1179656 | tf_op jit(solution)/shard_map/ppermute | solution.py:19
  644.1 7.2 collective-permute-start.2
  647.2 8.4 %collective-permute-start.3 = (f32[22,3,512]{2,1,0:T(4,128)S(1)}, f32[22,3,512]{2,1,0:T(4,128)S(1)}, u32[]{:S(2)}, u32[]{:S(2)}) collective-permute-start(f32[22,3,512]{2,1,0:T(4,128)S(1)} %get-tuple-element.53), channel_id=1, source_target_pairs={{1,0},{2,1},{3,2},{4,3},{5,4},{6,5},{7,6},{9,8},{10,9},{11,10},{12... | collective-permute-start | bytes 405512 | tf_op jit(solution)/shard_map/ppermute | solution.py:19
  690.0 24.8 %slice-start.6 = ((s8[4587520]{0:T(1024)(128)(4,1)}), s8[393216]{0:T(1024)(128)(4,1)S(1)}, s32[]{:S(2)}) async-start(s8[4587520]{0:T(1024)(128)(4,1)} %bitcast.911), calls=%async_computation.14 | async-start | bytes 786432
  692.6 22.2 %slice-start.7 = ((s8[4587520]{0:T(1024)(128)(4,1)}), s8[4194304]{0:T(1024)(128)(4,1)S(1)}, s32[]{:S(2)}) async-start(s8[4587520]{0:T(1024)(128)(4,1)} %bitcast.911), calls=%async_computation.15 | async-start | bytes 8388608
  702.9 21.3 %slice-start.4 = ((s8[4587520]{0:T(1024)(128)(4,1)}), s8[4194304]{0:T(1024)(128)(4,1)S(1)}, s32[]{:S(2)}) async-start(s8[4587520]{0:T(1024)(128)(4,1)} %bitcast.909), calls=%async_computation.12 | async-start | bytes 8388608
  702.9 31.2 %slice-start.2 = ((s8[4587520]{0:T(1024)(128)(4,1)}), s8[4194304]{0:T(1024)(128)(4,1)S(1)}, s32[]{:S(2)}) async-start(s8[4587520]{0:T(1024)(128)(4,1)} %bitcast.907), calls=%async_computation.10 | async-start | bytes 8388608
  (28 other events, 274.9 us)
Sparse Core Ops, SparseCore 0:
  32.3 54.9 all-gather.16
  104.9 52.3 all-gather.18
  181.1 52.3 all-gather.20
  255.0 52.3 all-gather.22
  331.2 52.4 all-gather.24
  405.0 52.3 all-gather.26
  481.2 52.4 all-gather.28
  557.8 52.4 all-gather.30
